TPU v7x, 256 devices: a whole 4x4x8 slice. The times are simulated.
256 devices in a mesh: pipe: 8 (over x, core), ctx: 16 (over z_hi, y), tp: 2 (over z_lo).
Axes of the slice: x: 4, y: 4, z: 8 (z_hi: 4, z_lo: 2; z = z_hi * 2 + z_lo), core: 2. Of those that a mesh axis runs over, the one named last changes fastest.
Arguments:
- qkv_proj: bfloat16 [8, 3, 2048, 8192], P('pipe', None, 'ctx', 'tp'), may hold values from -6 to 6
- cotangent: bfloat16 [8, 2048, 8192], P('pipe', 'ctx', 'tp'), may hold values from -6 to 6
- block_dest: int32 [8, 256], replicated, may hold values from 0 to 255, as said below
- doc_start: int32 [8, 2048], P('pipe', 'ctx'), may hold values 0 or 1
- mr_filter: bfloat16 [8, 512, 128], P('pipe', 'tp'), may hold values from -0.5 to 0.5
Outputs:
- input_grads: bfloat16 [8, 3, 2048, 8192], P('pipe', None, ('ctx', 'tp'))
Inputs may be any that keep to these rules, and one draw needn't show every extreme that they name: For each section p, block_dest[p] is a permutation of 0 .. 255. Entry d * 16 + b belongs to block b of ctx index d, and its value lies in b * 16 .. b * 16 + 15: every ctx index sends its block b to the part of the sequence held by ctx index b.
All inputs are finite; a program needn't handle non-finite values. No bound on the sum of `doc_start` on one device may be relied on, other than what follows from the above.
Results may differ from a plain program's by a relative error of at most 0.0049.
Values may be sent and summed in bfloat16 or wider, within the bound.
A program may use at most 128 MiB of HBM per device.

v0:
```python
import math

import jax
import jax.numpy as jnp
from jax import lax
from jax.sharding import PartitionSpec as P


def passed_along(block, axis, distance):
    devices = range(lax.axis_size(axis))
    route = [(i - distance, i) for i in devices if i - distance in devices]
    return lax.ppermute(block, axis, route)


def from_behind(array, axis, by):
    peers = lax.axis_size(axis)
    return lax.ppermute(array, axis, [(i, (i + by) % peers) for i in range(peers)])


def banded(filt, tile_rows):
    group_count, tap_count = filt.shape
    span_cols = tile_rows + tap_count - 1
    lag_grid = (
        jnp.arange(span_cols, dtype=jnp.int32)[None, :]
        - jnp.arange(tile_rows, dtype=jnp.int32)[:, None]
    )
    tap_ids = jnp.arange(tap_count, dtype=jnp.int32)
    one_hot = (
        (lag_grid[None, :, :] == tap_ids[:, None, None])
        .astype(filt.dtype)
        .reshape(tap_count, tile_rows * span_cols)
    )
    spread = jnp.dot(filt, one_hot, preferred_element_type=jnp.float32).astype(filt.dtype)
    return spread.reshape(group_count, tile_rows, span_cols)


def grouped_conv(filt, source, seg_out, seg_in):
    group_count, tap_count = filt.shape
    channels = source.shape[1]
    row_count = seg_out.shape[0]
    group_size = channels // group_count
    tile_rows = math.gcd(row_count, 64)
    span_rows = tile_rows + tap_count - 1
    toeplitz = banded(filt, tile_rows)
    results = []
    for row_first in range(0, row_count, tile_rows):
        window = source[row_first : row_first + span_rows].reshape(
            span_rows, group_count, group_size
        )
        seg_window = seg_in[row_first : row_first + span_rows]
        seg_target = seg_out[row_first : row_first + tile_rows]
        same_doc = (seg_window[None, :] == seg_target[:, None]).astype(filt.dtype)
        masked = toeplitz * same_doc[None]
        product = jnp.einsum("gts,sgc->tgc", masked, window, preferred_element_type=jnp.float32)
        results.append(product.reshape(tile_rows, channels))
    return jnp.concatenate(results, axis=0)


def placement_of(routes, target, ctx_count):
    column = lax.dynamic_index_in_dim(routes, target, 1, keepdims=False)
    slot_of_source = column % ctx_count
    peer_ids = jnp.arange(ctx_count, dtype=jnp.int32)
    source_of_slot = jnp.sum(
        jnp.where(slot_of_source[None, :] == peer_ids[:, None], peer_ids[None, :], 0), axis=1
    )
    return (slot_of_source, source_of_slot)


def shards(qkv_proj, cotangent, block_dest, doc_start, mr_filter):
    ctx_count = lax.axis_size("ctx")
    ctx_index = lax.axis_index("ctx")
    pipe_index = lax.axis_index("pipe")
    projected = qkv_proj[0]
    grad_arrival = cotangent[0]
    marks_arrival = doc_start[0]
    medium_taps = mr_filter[0]
    rim_rows = medium_taps.shape[1] - 1
    row_count, channels = grad_arrival.shape
    block_rows = row_count // ctx_count
    routes = lax.dynamic_index_in_dim(block_dest, pipe_index, 0, keepdims=False).reshape(
        ctx_count, ctx_count
    )
    slot_of_source, source_of_slot = placement_of(routes, ctx_index, ctx_count)
    proj_blocks = projected.reshape(3, ctx_count, block_rows, channels)
    grad_blocks = grad_arrival.reshape(1, ctx_count, block_rows, channels)
    mark_blocks = marks_arrival.reshape(1, ctx_count, block_rows)
    got_proj, got_grad, got_marks = (
        lax.all_to_all(proj_blocks, "ctx", split_axis=1, concat_axis=1, tiled=True),
        lax.all_to_all(grad_blocks, "ctx", split_axis=1, concat_axis=1, tiled=True),
        lax.all_to_all(mark_blocks, "ctx", split_axis=1, concat_axis=1, tiled=True),
    )
    seq_proj = jnp.take(got_proj, source_of_slot, axis=1).reshape(3, row_count, channels)
    grad_in = jnp.take(got_grad, source_of_slot, axis=1).reshape(row_count, channels)
    seq_marks = jnp.take(got_marks, source_of_slot, axis=1).reshape(row_count)
    query = seq_proj[0]
    key_rows = seq_proj[1]
    value = seq_proj[2]
    mixed = (key_rows.astype(jnp.float32) * value.astype(jnp.float32)).astype(jnp.bfloat16)
    past_mixed, past_marks = passed_along(
        (mixed[row_count - rim_rows :], seq_marks[row_count - rim_rows :]), "ctx", 1
    )
    gate_grad = (grad_in.astype(jnp.float32) * query.astype(jnp.float32)).astype(jnp.bfloat16)
    next_grad, next_marks = passed_along((gate_grad[:rim_rows], seq_marks[:rim_rows]), "ctx", -1)
    segment = jnp.cumsum(jnp.concatenate([past_marks, seq_marks, next_marks]), dtype=jnp.int32)
    seg_here = segment[rim_rows : rim_rows + row_count]
    mixed_ext = jnp.concatenate([past_mixed, mixed], axis=0)
    medium = grouped_conv(
        medium_taps[:, ::-1], mixed_ext, seg_here, segment[: row_count + rim_rows]
    )
    grad_ext = jnp.concatenate([gate_grad, next_grad], axis=0)
    mixed_grad = grouped_conv(medium_taps, grad_ext, seg_here, segment[rim_rows:])
    d_query = (grad_in.astype(jnp.float32) * medium).astype(jnp.bfloat16)
    d_key = (mixed_grad * value.astype(jnp.float32)).astype(jnp.bfloat16)
    d_value = (mixed_grad * key_rows.astype(jnp.float32)).astype(jnp.bfloat16)
    seq_out = jnp.stack([d_query, d_key, d_value]).reshape(3, ctx_count, block_rows, channels)
    outgoing = jnp.take(seq_out, slot_of_source, axis=1)
    returned = lax.all_to_all(
        lax.all_to_all(outgoing, "ctx", split_axis=1, concat_axis=1, tiled=True),
        "tp",
        split_axis=1,
        concat_axis=3,
        tiled=True,
    )
    moved = from_behind(returned, "pipe", -1)
    return moved.reshape(1, 3, -1, moved.shape[3])


def solution(mesh):
    placed = (
        P("pipe", None, "ctx", "tp"),
        P("pipe", "ctx", "tp"),
        P(),
        P("pipe", "ctx"),
        P("pipe", "tp", None),
    )
    return jax.shard_map(
        shards,
        mesh=mesh,
        in_specs=placed,
        out_specs=P("pipe", None, ("ctx", "tp"), None),
        check_vma=False,
    )
```

profile of v0, /device:TPU:1, one launch (start us, length us, event | category | flops | bytes accessed | tf_op | source)
XLA Modules:
  0.0 457.3 jit_solution(16317548914194845109)
XLA Ops:
  1.9 20.4 %all_to_all.38 = s32[1,16,8]{2,0,1:T(1,128)S(1)} all-to-all(s32[1,16,8]{2,0,1:T(1,128)S(1)} %bitcast.112), channel_id=1, replica_groups=mesh['pipe'=8,'ctx'=16,'tp'=2] {'ctx'}, dimensions={1} | all-to-all | bytes 1024 | tf_op jit(solution)/shard_map/all_to_all | solution.py:90
  22.3 3.7 all-to-all-start
  25.9 3.9 copy.95
  29.9 20.4 %all-to-all-done = bf16[1,16,8,4096]{3,2,0,1:T(8,128)(2,1)S(1)} async-done(((bf16[1,16,8,4096]{3,2,0,1:T(8,128)(2,1)}), bf16[1,16,8,4096]{3,2,0,1:T(8,128)(2,1)S(1)}, u32[]{:S(2)}, u32[]{:S(2)}) %all-to-all-start) | async-done | bytes 1048608 | tf_op jit(solution)/shard_map/all_to_all | solution.py:89
  51.3 7.6 %all-to-all-start.1 = ((bf16[3,16,8,4096]{3,2,0,1:T(8,128)(2,1)}), bf16[3,16,8,4096]{3,2,0,1:T(8,128)(2,1)S(1)}, u32[]{:S(2)}, u32[]{:S(2)}) async-start(bf16[3,16,8,4096]{3,2,0,1:T(8,128)(2,1)} %copy.95), calls=%async_computation.1 | async-start | bytes 6291456 | tf_op jit(solution)/shard_map/all_to_all | solution.py:88
  59.8 4.5 fusion.1
  65.0 3.2 collective-permute-start.1
  69.6 8.5 %reshape.294 = bf16[256,64,191]{0,2,1:T(8,128)(2,1)} reshape(bf16[256,12224]{0,1:T(8,128)(2,1)} %fusion.1) | data formatting | bytes 12517376 | tf_op jit(solution)/shard_map/reshape | solution.py:34
  82.1 32.9 %all-to-all-done.1 = bf16[3,16,8,4096]{3,2,0,1:T(8,128)(2,1)S(1)} async-done(((bf16[3,16,8,4096]{3,2,0,1:T(8,128)(2,1)}), bf16[3,16,8,4096]{3,2,0,1:T(8,128)(2,1)S(1)}, u32[]{:S(2)}, u32[]{:S(2)}) %all-to-all-start.1) | async-done | bytes 3145760 | tf_op jit(solution)/shard_map/all_to_all | solution.py:88
  116.9 4.5 gather_fusion.2
  125.9 7.0 %broadcast_multiply_fusion.1 = (bf16[256,64,191]{0,2,1:T(8,128)(2,1)}, bf16[256,64,191]{0,2,1:T(8,128)(2,1)}) fusion(bf16[256,64,191]{0,2,1:T(8,128)(2,1)S(1)} %bitcast.94, bf16[64,191]{1,0:T(8,128)(2,1)S(1)} %get-tuple-element.31, bf16[64,191]{1,0:T(8,128)(2,1)S(1)} %get-tuple-element.28), kind=kLoop, calls=%fused_computation.15 | loop fusion | flops 6258688 | bytes 18824960 | tf_op jit(solution)/shard_map/mul | solution.py:53
  132.9 12.1 %copy.108 = bf16[256,64,191]{2,1,0:T(8,128)(2,1)} copy(bf16[256,64,191]{0,2,1:T(8,128)(2,1)} %get-tuple-element.10) | data formatting | bytes 12517376 | tf_op jit(solution)/shard_map/mul | solution.py:53
  145.0 12.1 %copy.110 = bf16[256,64,191]{2,1,0:T(8,128)(2,1)} copy(bf16[256,64,191]{0,2,1:T(8,128)(2,1)} %get-tuple-element.11) | data formatting | bytes 12517376 | tf_op jit(solution)/shard_map/mul | solution.py:53
  157.1 3.5 fusion.13
  163.7 7.0 %fusion.24 = f32[256,16,64]{2,1,0:T(8,128)} fusion(bf16[191,256,16]{0,2,1:T(8,128)(2,1)S(1)} %bitcast.97, bf16[256,64,191]{2,1,0:T(8,128)(2,1)} %copy.108), kind=kOutput, calls=%fused_computation.77 | convolution fusion | flops 100139008 | bytes 8871936 | tf_op jit(solution)/shard_map/gts,sgc->tgc/dot_general | solution.py:54
  170.7 3.2 copy.111
  177.0 7.1 %fusion.25 = f32[256,16,64]{2,1,0:T(8,128)} fusion(bf16[191,256,16]{0,2,1:T(8,128)(2,1)S(1)} %bitcast.98, bf16[256,64,191]{2,1,0:T(8,128)(2,1)} %copy.110), kind=kOutput, calls=%fused_computation.78 | convolution fusion | flops 100139008 | bytes 8871936 | tf_op jit(solution)/shard_map/gts,sgc->tgc/dot_general | solution.py:54
  184.1 3.4 copy.112
  187.4 3.7 fusion.9
  192.3 4.3 collective-permute-start
  196.6 4.5 fusion
  201.1 8.5 %reshape.289 = bf16[256,64,191]{0,2,1:T(8,128)(2,1)} reshape(bf16[256,12224]{0,1:T(8,128)(2,1)} %fusion) | data formatting | bytes 12517376 | tf_op jit(solution)/shard_map/reshape | solution.py:34
  209.6 9.9 %broadcast_multiply_fusion.3 = (bf16[256,64,191]{0,2,1:T(8,128)(2,1)}, bf16[256,64,191]{0,2,1:T(8,128)(2,1)}) fusion(bf16[256,64,191]{0,2,1:T(8,128)(2,1)} %reshape.289, bf16[64,191]{1,0:T(8,128)(2,1)S(1)} %get-tuple-element.32, bf16[64,191]{1,0:T(8,128)(2,1)S(1)} %get-tuple-element.27), kind=kLoop, calls=%fused_computation.17 | loop fusion | flops 6258688 | bytes 18824960 | tf_op jit(solution)/shard_map/mul | solution.py:53
  219.4 12.1 %copy.101 = bf16[256,64,191]{2,1,0:T(8,128)(2,1)} copy(bf16[256,64,191]{0,2,1:T(8,128)(2,1)} %get-tuple-element.8) | data formatting | bytes 12517376 | tf_op jit(solution)/shard_map/mul | solution.py:53
  231.5 12.2 %copy.103 = bf16[256,64,191]{2,1,0:T(8,128)(2,1)} copy(bf16[256,64,191]{0,2,1:T(8,128)(2,1)} %get-tuple-element.9) | data formatting | bytes 12517376 | tf_op jit(solution)/shard_map/mul | solution.py:53
  249.0 7.0 %fusion.22 = f32[256,16,64]{2,1,0:T(8,128)} fusion(bf16[191,256,16]{0,2,1:T(8,128)(2,1)S(1)} %bitcast.99, bf16[256,64,191]{2,1,0:T(8,128)(2,1)} %copy.101), kind=kOutput, calls=%fused_computation.75 | convolution fusion | flops 100139008 | bytes 8871936 | tf_op jit(solution)/shard_map/gts,sgc->tgc/dot_general | solution.py:54
  261.3 7.0 %fusion.23 = f32[256,16,64]{2,1,0:T(8,128)} fusion(bf16[191,256,16]{0,2,1:T(8,128)(2,1)S(1)} %bitcast.100, bf16[256,64,191]{2,1,0:T(8,128)(2,1)} %copy.103), kind=kOutput, calls=%fused_computation.76 | convolution fusion | flops 100139008 | bytes 8871936 | tf_op jit(solution)/shard_map/gts,sgc->tgc/dot_general | solution.py:54
  277.1 48.4 %all_to_all.39 = bf16[3,16,8,4096]{3,2,0,1:T(8,128)(2,1)S(1)} all-to-all(bf16[3,16,8,4096]{3,2,0,1:T(8,128)(2,1)S(1)} %select_bitcast_fusion), channel_id=1, replica_groups=mesh['pipe'=8,'ctx'=16,'tp'=2] {'ctx'}, dimensions={1} | all-to-all | bytes 6291456 | tf_op jit(solution)/shard_map/all_to_all | solution.py:118
  325.5 85.3 %all_to_all.40 = bf16[3,16,8,4096]{3,2,0,1:T(8,128)(2,1)S(1)} all-to-all(bf16[3,16,8,4096]{3,2,0,1:T(8,128)(2,1)S(1)} %all_to_all.39), channel_id=1, replica_groups=mesh['pipe'=8,'ctx'=16,'tp'=2] {'tp'}, dimensions={1} | all-to-all | bytes 6291456 | tf_op jit(solution)/shard_map/all_to_all | solution.py:117
  410.8 3.3 copy.118
  414.1 4.0 all_to_all.32
  419.4 36.3 %collective-permute-done.4 = bf16[3,8,8,8192]{3,2,1,0:T(8,128)(2,1)S(1)} collective-permute-done((bf16[3,8,8,8192]{3,2,1,0:T(8,128)(2,1)}, bf16[3,8,8,8192]{3,2,1,0:T(8,128)(2,1)S(1)}, u32[]{:S(2)}, u32[]{:S(2)}) %collective-permute-start.4) | collective-permute-done | bytes 3145760 | tf_op jit(solution)/shard_map/ppermute | solution.py:17
  (89 shorter events, 46.1 us)
Async XLA Ops:
  0.0 58.9 %copy-start = (s32[8,256]{1,0:T(8,128)S(1)}, s32[8,256]{1,0:T(8,128)}, u32[]{:S(2)}) copy-start(s32[8,256]{1,0:T(8,128)} %param.9) | copy-start | bytes 24580
  22.3 28.0 %all-to-all-start = ((bf16[1,16,8,4096]{3,2,0,1:T(8,128)(2,1)}), bf16[1,16,8,4096]{3,2,0,1:T(8,128)(2,1)S(1)}, u32[]{:S(2)}, u32[]{:S(2)}) async-start(bf16[1,16,8,4096]{3,2,0,1:T(8,128)(2,1)} %bitcast.109), calls=%async_computation | async-start | bytes 2097152 | tf_op jit(solution)/shard_map/all_to_all | solution.py:89
  29.9 29.9 %copy-start.11 = (bf16[1,256,128]{2,1,0:T(8,128)(2,1)S(1)}, bf16[1,256,128]{2,1,0:T(8,128)(2,1)}, u32[]{:S(2)}) copy-start(bf16[1,256,128]{2,1,0:T(8,128)(2,1)} %param.11) | copy-start | bytes 196612
  50.2 1.1 copy-start.8
  51.3 63.7 %all-to-all-start.1 = ((bf16[3,16,8,4096]{3,2,0,1:T(8,128)(2,1)}), bf16[3,16,8,4096]{3,2,0,1:T(8,128)(2,1)S(1)}, u32[]{:S(2)}, u32[]{:S(2)}) async-start(bf16[3,16,8,4096]{3,2,0,1:T(8,128)(2,1)} %copy.95), calls=%async_computation.1 | async-start | bytes 6291456 | tf_op jit(solution)/shard_map/all_to_all | solution.py:88
  65.0 13.5 %collective-permute-start.1 = (s32[127]{0:T(128)S(1)}, s32[127]{0:T(128)S(1)}, u32[]{:S(2)}, u32[]{:S(2)}) collective-permute-start(s32[127]{0:T(128)S(1)} %get-tuple-element.29), channel_id=1, source_target_pairs={{0,2},{2,4},{4,6},{6,8},{8,10},{10,12},{12,14},{14,16},{16,18},{18... | collective-permute-start | bytes 1532 | tf_op jit(solution)/shard_map/ppermute | solution.py:12
  68.2 10.2 %collective-permute-start.2 = (s32[127]{0:T(128)S(1)}, s32[127]{0:T(128)S(1)}, u32[]{:S(2)}, u32[]{:S(2)}) collective-permute-start(s32[127]{0:T(128)S(1)} %get-tuple-element.30), channel_id=1, source_target_pairs={{2,0},{4,2},{6,4},{8,6},{10,8},{12,10},{14,12},{16,14},{18,16},{20... | collective-permute-start | bytes 1532 | tf_op jit(solution)/shard_map/ppermute | solution.py:12
  116.9 9.0 %slice-start = ((s8[6291456]{0:T(1024)(128)(4,1)}), s8[2097152]{0:T(1024)(128)(4,1)S(1)}, s32[]{:S(2)}) async-start(s8[6291456]{0:T(1024)(128)(4,1)} %bitcast.93), calls=%async_computation.5 | async-start | bytes 4194304
  121.4 2.4 copy-start.6
  121.4 4.5 slice-start.1
  123.8 9.1 %copy-start.2 = (bf16[3,16,8,4096]{3,2,0,1:T(8,128)(2,1)}, bf16[3,16,8,4096]{3,2,0,1:T(8,128)(2,1)S(1)}, u32[]{:S(2)}) copy-start(bf16[3,16,8,4096]{3,2,0,1:T(8,128)(2,1)S(1)} %select_bitcast_fusion.1) | copy-start | bytes 9437188
  124.2 32.9 %collective-permute-start.3 = (bf16[127,4096]{1,0:T(8,128)(2,1)S(1)}, bf16[127,4096]{1,0:T(8,128)(2,1)}, u32[]{:S(2)}, u32[]{:S(2)}) collective-permute-start(bf16[127,4096]{1,0:T(8,128)(2,1)S(1)} %bitcast.105), channel_id=1, source_target_pairs={{2,0},{4,2},{6,4},{8,6},{10,8},{12,10},{14,12},{16,14},{18,16},{20... | collective-permute-start | bytes 3121160 | tf_op jit(solution)/shard_map/ppermute | solution.py:12
  184.1 3.4 copy-start.3
  191.1 1.0 copy-start.4
  192.3 51.4 %collective-permute-start = (bf16[127,4096]{1,0:T(8,128)(2,1)S(1)}, bf16[127,4096]{1,0:T(8,128)(2,1)S(1)}, u32[]{:S(2)}, u32[]{:S(2)}) collective-permute-start(bf16[127,4096]{1,0:T(8,128)(2,1)S(1)} %slice.105), channel_id=1, source_target_pairs={{0,2},{2,4},{4,6},{6,8},{8,10},{10,12},{12,14},{14,16},{16,18},{18... | collective-permute-start | bytes 3121160 | tf_op jit(solution)/shard_map/ppermute | solution.py:12
  231.5 12.2 %copy-start.5 = (bf16[128,4096]{1,0:T(8,128)(2,1)S(1)}, bf16[128,4096]{1,0:T(8,128)(2,1)}, u32[]{:S(2)}) copy-start(bf16[128,4096]{1,0:T(8,128)(2,1)} %copy-done.4) | copy-start | bytes 3145732
  268.3 2.3 copy-start.7
  270.6 1.2 copy-start.9
  270.6 1.5 copy-start.10
  418.1 37.6 %collective-permute-start.4 = (bf16[3,8,8,8192]{3,2,1,0:T(8,128)(2,1)}, bf16[3,8,8,8192]{3,2,1,0:T(8,128)(2,1)S(1)}, u32[]{:S(2)}, u32[]{:S(2)}) collective-permute-start(bf16[3,8,8,8192]{3,2,1,0:T(8,128)(2,1)} %all_to_all.32), channel_id=1, source_target_pairs={{0,224},{32,0},{64,32},{96,64},{128,96},{160,128},{192,160},{224,1... | collective-permute-start | bytes 9437192 | tf_op jit(solution)/shard_map/ppermute | solution.py:17
  455.7 1.7 copy-start.1
where the time goes:
time: 460 us; the launch traced here: 457 us
  blocking collectives  154 us (33%)
  local copies, waits for them, and re-layouts  120 us (26%)
  waiting for transfers between devices  89.5 us (19%)
  matrix products  37 us (8%)
  other arithmetic  33.9 us (7%)
  starting transfers between devices  22.9 us (5%)
    all_to_all x1, blocking collectives, shards(): lax.all_to_all(lax.all_to_all(outgoing, 'ctx', split_axis=1, concat_axis=...  85.3 us
    mul x4, local copies, waits for them, and re-layouts, grouped_conv(): masked = toeplitz * same_doc[None]  48.4 us
    all_to_all x1, blocking collectives, shards(): lax.all_to_all(outgoing, 'ctx', split_axis=1, concat_axis=1, tiled=True)  48.4 us
    ppermute x1, waiting for transfers between devices, from_behind(): lax.ppermute(array, axis, [(i, (i + by) % peers) for i in range(peers)])  36.3 us
    all_to_all x1, waiting for transfers between devices, shards(): lax.all_to_all(proj_blocks, 'ctx', split_axis=1, concat_axis=1, tiled=True)  32.9 us
    dot_general x4, matrix products, grouped_conv(): jnp.einsum('gts,sgc->tgc', masked, window, preferred_element_type=jnp.flo...  28.1 us
    all_to_all x1, waiting for transfers between devices, shards(): lax.all_to_all(grad_blocks, 'ctx', split_axis=1, concat_axis=1, tiled=True)  20.4 us
    all_to_all x1, blocking collectives, shards(): lax.all_to_all(mark_blocks, 'ctx', split_axis=1, concat_axis=1, tiled=True)  20.4 us
  transfers between devices with their start and end apart: 7, of which 3 were waited for; matrix products, arithmetic and copies ran while one was open for 22% of the time, Pallas kernels for 0%

commit v1 on v0

v1 whole, which is shorter than its diff:
```python
import functools

import jax
import jax.numpy as jnp
from jax import lax
from jax.experimental import pallas as pl
from jax.experimental.pallas import tpu as pltpu
from jax.sharding import PartitionSpec as P

MESH = pl.DeviceIdType.MESH
F32 = jnp.float32
BF16 = jnp.bfloat16
LANES = 128
STAGES = 4


def iota(shape, dim):
    return lax.broadcasted_iota(jnp.int32, shape, dim)


def dot(a, b):
    return jnp.dot(a, b, preferred_element_type=F32)


def await_bytes(ref, sem):
    pltpu.make_async_copy(ref, ref, sem).wait()


def kernel(
    sizes,
    qkv_ref,
    cot_ref,
    dest_ref,
    marks_ref,
    filt_ref,
    out_ref,
    raw,
    stage,
    got,
    marks_all,
    taps,
    bands,
    pos_all,
    counts,
    masks,
    to_seq,
    to_arrival,
    source,
    outgoing,
    final,
    factors,
    load_sem,
    stage_send,
    stage_recv,
    mark_send,
    mark_recv,
    factor_send,
    factor_recv,
    final_send,
    final_recv,
):
    pipes, ctxs, tps = sizes
    p, c, t = lax.axis_index("pipe"), lax.axis_index("ctx"), lax.axis_index("tp")
    behind = lax.rem(p + pipes - 1, pipes)
    ahead = lax.rem(p + 1, pipes)
    rows = raw.shape[1]
    half_rows = rows // tps
    groups = taps.shape[1]
    stage_groups = groups // 2
    group_size = LANES // stage_groups

    barrier = pltpu.get_barrier_semaphore()
    for j in range(1, ctxs):
        peer = (p, lax.rem(c + j, ctxs), t)
        pl.semaphore_signal(barrier, inc=1, device_id=peer, device_id_type=MESH)
    for j in range(ctxs):
        for k in range(tps):
            peer = (ahead, lax.rem(c + j, ctxs), k)
            pl.semaphore_signal(barrier, inc=1, device_id=peer, device_id_type=MESH)

    loads = []
    for i, ref in enumerate((cot_ref.at[0], qkv_ref.at[0, 0], qkv_ref.at[0, 1], qkv_ref.at[0, 2])):
        load = pltpu.make_async_copy(ref, raw.at[i], load_sem.at[i])
        load.start()
        loads.append(load)

    def products(s):
        first, second, half = 2 * (s // 2), 2 * (s // 2) + 1, s % 2

        def one(j, carry):
            col = pl.multiple_of(j * (2 * LANES) + half * LANES, LANES)
            a = raw[first, :, pl.ds(col, LANES)].astype(F32)
            b = raw[second, :, pl.ds(col, LANES)].astype(F32)
            stage[s, j] = (a * b).reshape(rows // 8, 8, LANES).astype(BF16)
            return carry

        lax.fori_loop(0, ctxs, one, 0)

    def stage_copy(s, j):
        target = lax.rem(c + j, ctxs)
        return pltpu.make_async_remote_copy(
            src_ref=stage.at[s, target],
            dst_ref=got.at[s, c],
            send_sem=stage_send.at[s],
            recv_sem=stage_recv.at[s],
            device_id=(p, target, t),
            device_id_type=MESH,
        )

    def send_stage(s):
        for j in range(1, ctxs):
            stage_copy(s, j).start()
        got[s, c] = stage[s, c]

    loads[0].wait()
    loads[1].wait()
    products(0)
    pl.semaphore_wait(barrier, ctxs - 1 + ctxs * tps)
    for j in range(1, ctxs):
        pltpu.make_async_remote_copy(
            src_ref=marks_ref,
            dst_ref=marks_all.at[pl.ds(c, 1)],
            send_sem=mark_send,
            recv_sem=mark_recv,
            device_id=(p, lax.rem(c + j, ctxs), t),
            device_id_type=MESH,
        ).start()
    marks_all[pl.ds(c, 1)] = marks_ref[...]
    send_stage(0)
    products(1)
    send_stage(1)
    loads[2].wait()
    loads[3].wait()
    products(2)
    send_stage(2)
    products(3)
    send_stage(3)

    def factor_copies():
        copies = []
        for k in range(tps):
            span = pl.ds(k * half_rows, half_rows)
            for i, ref in enumerate((cot_ref.at[0], qkv_ref.at[0, 1], qkv_ref.at[0, 2])):
                copies.append(
                    pltpu.make_async_remote_copy(
                        src_ref=ref.at[span],
                        dst_ref=factors.at[t, i],
                        send_sem=factor_send,
                        recv_sem=factor_recv,
                        device_id=(behind, c, k),
                        device_id_type=MESH,
                    )
                )
        return copies

    mine = filt_ref[0, pl.ds(pl.multiple_of(c * groups, groups), groups), :]
    lag, lane = iota((LANES, 2 * LANES), 0), iota((LANES, 2 * LANES), 1)
    taps[0] = dot(mine, (lane == LANES - lag).astype(BF16))
    taps[1] = dot(mine, (lane == lag).astype(BF16))

    def one_band(i, carry):
        for way in range(2):
            row = jnp.broadcast_to(taps[way, pl.ds(i, 1), :], (LANES, 2 * LANES))
            band = pltpu.roll(row, 0, 1, stride=1, stride_axis=0)
            bands[way, i] = band.astype(BF16)
        return carry

    lax.fori_loop(0, groups, one_band, 0)

    slots = ctxs * ctxs
    dest = jnp.broadcast_to(dest_ref[pl.ds(p, 1), :], (ctxs, slots))
    entry, tile = iota((ctxs, slots), 1), iota((ctxs, slots), 0)
    slot = jnp.where(entry % ctxs == tile, dest - tile * ctxs, 0).astype(F32).astype(BF16)
    spread = (iota((slots, LANES), 0) // ctxs == iota((slots, LANES), 1) // 8).astype(BF16)
    pos_all[...] = dot(slot, spread) * 8.0 + (iota((ctxs, LANES), 1) % 8).astype(F32)

    await_bytes(marks_all.at[pl.ds(0, ctxs - 1)], mark_recv)
    down = iota((LANES, LANES), 0)
    across = iota((LANES, LANES), 1)
    owner = iota((ctxs, LANES), 0) == iota((ctxs, LANES), 1) // 8

    def one_order(b, table):
        pick = (down == b * 8 + across % 8).astype(BF16)
        marks = dot(marks_all[...].astype(F32).astype(BF16), pick)
        marks = jnp.sum(jnp.where(owner, marks, 0.0), axis=0, keepdims=True)
        pos = pos_all[pl.ds(b, 1), :]
        rank = down.astype(F32)
        place = (pos == rank).astype(F32)
        to_seq[b] = place.astype(BF16)
        to_arrival[b] = place.T.astype(BF16)
        count = jnp.sum(jnp.where(pos <= rank, marks, 0.0), axis=1, keepdims=True)
        return jnp.where(across == b, count, table)

    table = lax.fori_loop(0, ctxs, one_order, jnp.zeros((LANES, LANES), F32))
    counts[...] = table.T

    def one_mask(b, carry):
        here = counts[pl.ds(b, 1), :]
        total = here[:, LANES - 1 :]
        prior = counts[pl.ds(jnp.maximum(b - 1, 0), 1), :]
        prior = jnp.where(b > 0, prior - prior[:, LANES - 1 :], -1.0)
        later = counts[pl.ds(jnp.minimum(b + 1, ctxs - 1), 1), :]
        later = jnp.where(b < ctxs - 1, later + total, -1.0)
        column = jnp.broadcast_to(here, (LANES, LANES)).T
        column = jnp.concatenate([column, column], axis=1)
        masks[0, b] = (column == jnp.concatenate([prior, here], axis=1)).astype(F32).astype(BF16)
        masks[1, b] = (column == jnp.concatenate([here, later], axis=1)).astype(F32).astype(BF16)
        return carry

    lax.fori_loop(0, ctxs, one_mask, 0)
    source[pl.ds(0, LANES), :] = jnp.zeros((LANES, LANES), BF16)
    source[pl.ds((ctxs + 1) * LANES, LANES), :] = jnp.zeros((LANES, LANES), BF16)
    group_of_lane = iota((LANES, LANES), 1) // group_size

    def convolve(s):
        way, half = 1 - s // 2, s % 2

        def order(b, carry):
            block = got[s, :, b].astype(F32).reshape(LANES, LANES).astype(BF16)
            at = pl.multiple_of((b + 1) * LANES, LANES)
            source[pl.ds(at, LANES), :] = dot(to_seq[b], block).astype(BF16)
            return carry

        lax.fori_loop(0, ctxs, order, 0)

        def one_tile(b, carry):
            window = source[pl.ds(pl.multiple_of((b + way) * LANES, LANES), 2 * LANES), :]
            mask = masks[way, b]
            total = jnp.zeros((LANES, LANES), F32)
            for g in range(stage_groups):
                band = bands[way, half * stage_groups + g] * mask
                total = jnp.where(group_of_lane == g, dot(band, window), total)
            back = dot(to_arrival[b], total.astype(BF16))
            outgoing[s, :, b] = back.reshape(ctxs, 8, LANES).astype(BF16)
            return carry

        lax.fori_loop(0, ctxs, one_tile, 0)

    def send_final(s):
        half_blocks = ctxs // tps
        for j in range(ctxs):
            target = lax.rem(c + j, ctxs)
            for k in range(tps):
                pltpu.make_async_remote_copy(
                    src_ref=outgoing.at[s, target, pl.ds(k * half_blocks, half_blocks)],
                    dst_ref=final.at[s, t, c],
                    send_sem=final_send.at[s],
                    recv_sem=final_recv.at[s],
                    device_id=(behind, target, k),
                    device_id_type=MESH,
                ).start()

    for s in range(STAGES):
        await_bytes(got.at[s, pl.ds(0, ctxs - 1)], stage_recv.at[s])
        convolve(s)
        send_final(s)
        if s == 0:
            for copy in factor_copies():
                copy.start()

    for copy in factor_copies():
        copy.wait_send()
    await_bytes(factors, factor_recv)

    def finish(s):
        half = s % 2

        def one(i, carry):
            side, peer = i // ctxs, i % ctxs
            near = pl.ds(pl.multiple_of(peer * (2 * LANES) + half * LANES, LANES), LANES)
            far = pl.ds(
                pl.multiple_of(side * (ctxs * 2 * LANES) + peer * (2 * LANES) + half * LANES, LANES),
                LANES,
            )
            conv = final[s, side, peer].astype(F32).reshape(half_rows, LANES)
            if s >= 2:
                out_ref[0, 0, :, far] = (factors[side, 0, :, near].astype(F32) * conv).astype(BF16)
            else:
                out_ref[0, 1, :, far] = (factors[side, 2, :, near].astype(F32) * conv).astype(BF16)
                out_ref[0, 2, :, far] = (factors[side, 1, :, near].astype(F32) * conv).astype(BF16)
            return carry

        lax.fori_loop(0, tps * ctxs, one, 0)

    for s in range(STAGES):
        await_bytes(final.at[s], final_recv.at[s])
        finish(s)

    await_bytes(marks_all.at[pl.ds(0, ctxs - 1)], mark_send)
    for s in range(STAGES):
        await_bytes(stage.at[s, pl.ds(0, ctxs - 1)], stage_send.at[s])
        await_bytes(outgoing.at[s], final_send.at[s])


def shards(sizes, qkv_proj, cotangent, block_dest, doc_start, mr_filter):
    pipes, ctxs, tps = sizes
    rows, channels = cotangent.shape[1:]
    taps = mr_filter.shape[2]
    groups = mr_filter.shape[1] // ctxs
    half_rows = rows // tps
    blocks = rows // 8
    dma = pltpu.SemaphoreType.DMA
    anywhere = pl.BlockSpec(memory_space=pl.ANY)
    vmem = pl.BlockSpec(memory_space=pltpu.VMEM)
    return pl.pallas_call(
        functools.partial(kernel, sizes),
        out_shape=jax.ShapeDtypeStruct((1, 3, half_rows, channels * tps), BF16),
        in_specs=[anywhere, anywhere, vmem, vmem, vmem],
        out_specs=vmem,
        scratch_shapes=[
            pltpu.VMEM((4, rows, channels), BF16),
            pltpu.VMEM((STAGES, ctxs, blocks, 8, LANES), BF16),
            pltpu.VMEM((STAGES, ctxs, blocks, 8, LANES), BF16),
            pltpu.VMEM((ctxs, LANES), jnp.int32),
            pltpu.VMEM((2, groups, 2 * taps), F32),
            pltpu.VMEM((2, groups, taps, 2 * taps), BF16),
            pltpu.VMEM((ctxs, LANES), F32),
            pltpu.VMEM((LANES, LANES), F32),
            pltpu.VMEM((2, ctxs, LANES, 2 * LANES), BF16),
            pltpu.VMEM((ctxs, LANES, LANES), BF16),
            pltpu.VMEM((ctxs, LANES, LANES), BF16),
            pltpu.VMEM(((ctxs + 2) * LANES, LANES), BF16),
            pltpu.VMEM((STAGES, ctxs, blocks, 8, LANES), BF16),
            pltpu.VMEM((STAGES, tps, ctxs, blocks // tps, 8, LANES), BF16),
            pltpu.VMEM((tps, 3, half_rows, channels), BF16),
            dma((4,)),
            dma((STAGES,)),
            dma((STAGES,)),
            dma,
            dma,
            dma,
            dma,
            dma((STAGES,)),
            dma((STAGES,)),
        ],
        compiler_params=pltpu.CompilerParams(
            collective_id=0, has_side_effects=True, vmem_limit_bytes=44 << 20
        ),
        name="hyena_input_grads",
    )(qkv_proj, cotangent, block_dest, doc_start, mr_filter)


def solution(mesh):
    sizes = (mesh.shape["pipe"], mesh.shape["ctx"], mesh.shape["tp"])
    placed = (
        P("pipe", None, "ctx", "tp"),
        P("pipe", "ctx", "tp"),
        P(),
        P("pipe", "ctx"),
        P("pipe", "tp", None),
    )
    return jax.shard_map(
        functools.partial(shards, sizes),
        mesh=mesh,
        in_specs=placed,
        out_specs=P("pipe", None, ("ctx", "tp"), None),
        check_vma=False,
    )
```

time: 460 us -> 146 us (0.32)
  blocking collectives: 154 us -> 0 us
  Pallas kernels: 0 us -> 139 us
  local copies, waits for them, and re-layouts: 120 us -> 6.97 us
  waiting for transfers between devices: 89.5 us -> 0 us
  matrix products: 37 us -> 0 us
  other arithmetic: 33.9 us -> 0 us
  starting transfers between devices: 22.9 us -> 0 us
    all_to_all x3 -> x0, blocking collectives: 154 us -> none  [the longest x1 85.3 us: shards(): lax.all_to_all(lax.all_to_all(outgoing, 'ctx', split_axis=1, concat_axis=...]
    pallas_call x0 -> x1, Pallas kernels: none -> 139 us  [shards(): pl.pallas_call(functools.partial(kernel, sizes), out_shape=jax.ShapeDtype...]
    all_to_all x2 -> x0, waiting for transfers between devices: 53.3 us -> none  [the longest x1 32.9 us: shards(): lax.all_to_all(proj_blocks, 'ctx', split_axis=1, concat_axis=1, tiled=True)]
    mul x4 -> x0, local copies, waits for them, and re-layouts: 48.4 us -> none  [grouped_conv(): masked = toeplitz * same_doc[None]]
    dot_general x6 -> x0, matrix products: 37 us -> none  [the longest x4 28.1 us: grouped_conv(): jnp.einsum('gts,sgc->tgc', masked, window, preferred_element_type=jnp.flo...]
    ppermute x5 -> x0, waiting for transfers between devices: 36.3 us -> none  [the longest x1 36.3 us: from_behind(): lax.ppermute(array, axis, [(i, (i + by) % peers) for i in range(peers)])]
    reshape x4 -> x0, local copies, waits for them, and re-layouts: 17.1 us -> none  [the longest x2 17 us: banded(): return spread.reshape(group_count, tile_rows, span_cols)]
    mul x2 -> x0, other arithmetic: 16.9 us -> none  [grouped_conv(): masked = toeplitz * same_doc[None]]
  transfers between devices with their start and end apart: 7 -> 0, of which waited for: 3 -> 0; matrix products, arithmetic and copies ran while one was open for 22% -> 0% of each run, Pallas kernels for 0% -> 0%
where the time goes in v1:
time: 146 us
  Pallas kernels  139 us (95%)
  local copies, waits for them, and re-layouts  6.97 us (5%)
    pallas_call x1, Pallas kernels, shards(): pl.pallas_call(functools.partial(kernel, sizes), out_shape=jax.ShapeDtype...  139 us
    unnamed x11, local copies, waits for them, and re-layouts  6.97 us

profile of v1, /device:TPU:1, one launch (start us, length us, event | category | flops | bytes accessed | tf_op | source)
XLA Modules:
  0.0 145.5 jit_solution(10140328195969128619)
XLA Ops:
  0.0 0.0 copy-start
  0.0 1.9 %copy-done = bf16[1,3,128,4096]{3,2,1,0:T(8,128)(2,1)S(1)} copy-done((bf16[1,3,128,4096]{3,2,1,0:T(8,128)(2,1)S(1)}, bf16[1,3,128,4096]{3,2,1,0:T(8,128)(2,1)}, u32[]{:S(2)}) %copy-start) | copy-done | bytes 3145752
  1.9 0.0 copy-start.1
  1.9 1.2 copy-done.1
  3.1 0.0 copy-start.2
  3.1 0.8 copy-done.2
  4.0 0.0 copy-start.3
  4.0 0.7 copy-done.3
  4.7 0.0 copy-start.4
  4.7 0.7 copy-done.4
  5.3 138.5 %hyena_input_grads.1 = bf16[1,3,64,8192]{3,2,1,0:T(8,128)(2,1)S(1)} custom-call(bf16[1,3,128,4096]{3,2,1,0:T(8,128)(2,1)S(1)} %copy-done, bf16[1,128,4096]{2,1,0:T(8,128)(2,1)S(1)} %copy-done.1, s32[8,256]{1,0:T(8,128)S(1)} %copy-done.3, s32[1,128]{1,0:T(1,128)S(1)} %copy-done.4, bf16[1,256,128]{2,1,0:T(8,128)(2,1)S(1)} %copy-done.2), custom_call_target="tpu_custom_call" | custom-call | tf_op jit(solution)/shard_map/hyena_input_grads/pallas_call | solution.py:305
  143.8 1.7 %copy.7 = bf16[1,3,64,8192]{3,2,1,0:T(8,128)(2,1)} copy(bf16[1,3,64,8192]{3,2,1,0:T(8,128)(2,1)S(1)} %hyena_input_grads.1) | data formatting | bytes 6291456
Async XLA Ops:
  0.0 1.9 %copy-start = (bf16[1,3,128,4096]{3,2,1,0:T(8,128)(2,1)S(1)}, bf16[1,3,128,4096]{3,2,1,0:T(8,128)(2,1)}, u32[]{:S(2)}) copy-start(bf16[1,3,128,4096]{3,2,1,0:T(8,128)(2,1)} %qkv_ref.1) | copy-start | bytes 9437188
  1.9 1.2 copy-start.1
  3.1 0.8 copy-start.2
  4.0 0.7 copy-start.3
  4.7 0.7 copy-start.4

commit v2 on v1

--- a/solution.py
+++ b/solution.py
@@ -12,6 +12,7 @@
 BF16 = jnp.bfloat16
 LANES = 128
 STAGES = 4
+RING = 4
 
 
 def iota(shape, dim):
@@ -48,7 +49,11 @@
     source,
     outgoing,
     final,
+    returned,
+    ready,
     factors,
+    dest_here,
+    filt_here,
     load_sem,
     stage_send,
     stage_recv,
@@ -58,6 +63,10 @@
     factor_recv,
     final_send,
     final_recv,
+    return_send,
+    return_recv,
+    ready_send,
+    ready_recv,
 ):
     pipes, ctxs, tps = sizes
     p, c, t = lax.axis_index("pipe"), lax.axis_index("ctx"), lax.axis_index("tp")
@@ -65,8 +74,16 @@
     ahead = lax.rem(p + 1, pipes)
     rows = raw.shape[1]
     half_rows = rows // tps
+    blocks = rows // 8
+    half_blocks = half_rows // 8
     groups = taps.shape[1]
     stage_groups = groups // 2
+    plane = ctxs // RING
+    deep, flat = c // plane, c % plane
+    sign = 1 - 2 * t
+    half_cols = ctxs * LANES
+    plane_cols = plane * LANES
+    crossing = pl.ds(pl.multiple_of((1 - t) * half_rows, half_rows), half_rows)
     group_size = LANES // stage_groups
 
     barrier = pltpu.get_barrier_semaphore()
@@ -79,8 +96,20 @@
             pl.semaphore_signal(barrier, inc=1, device_id=peer, device_id_type=MESH)
 
     loads = []
-    for i, ref in enumerate((cot_ref.at[0], qkv_ref.at[0, 0], qkv_ref.at[0, 1], qkv_ref.at[0, 2])):
-        load = pltpu.make_async_copy(ref, raw.at[i], load_sem.at[i])
+    first_group = pl.multiple_of(c * stage_groups, stage_groups)
+    for i, (source_ref, target_ref) in enumerate(
+        (
+            (cot_ref.at[0], raw.at[0]),
+            (qkv_ref.at[0, 0], raw.at[1]),
+            (qkv_ref.at[0, 1], raw.at[2]),
+            (qkv_ref.at[0, 2], raw.at[3]),
+            (dest_ref, dest_here),
+            (filt_ref.at[0, pl.ds(first_group, stage_groups)], filt_here.at[0]),
+            (filt_ref.at[0, pl.ds(ctxs * stage_groups + first_group, stage_groups)], filt_here.at[1]),
+            (marks_ref, marks_all.at[pl.ds(c, 1)]),
+        )
+    ):
+        load = pltpu.make_async_copy(source_ref, target_ref, load_sem.at[i])
         load.start()
         loads.append(load)
 
@@ -88,7 +117,7 @@
         first, second, half = 2 * (s // 2), 2 * (s // 2) + 1, s % 2
 
         def one(j, carry):
-            col = pl.multiple_of(j * (2 * LANES) + half * LANES, LANES)
+            col = pl.multiple_of(half * half_cols + j * LANES, LANES)
             a = raw[first, :, pl.ds(col, LANES)].astype(F32)
             b = raw[second, :, pl.ds(col, LANES)].astype(F32)
             stage[s, j] = (a * b).reshape(rows // 8, 8, LANES).astype(BF16)
@@ -125,7 +154,6 @@
             device_id=(p, lax.rem(c + j, ctxs), t),
             device_id_type=MESH,
         ).start()
-    marks_all[pl.ds(c, 1)] = marks_ref[...]
     send_stage(0)
     products(1)
     send_stage(1)
@@ -136,24 +164,47 @@
     products(3)
     send_stage(3)
 
-    def factor_copies():
+    arrays = (cot_ref.at[0], qkv_ref.at[0, 1], qkv_ref.at[0, 2])
+
+    def near_factors():
+        span = pl.ds(pl.multiple_of(t * half_rows, half_rows), half_rows)
+        return [
+            pltpu.make_async_remote_copy(
+                src_ref=ref.at[span],
+                dst_ref=factors.at[t, i],
+                send_sem=factor_send.at[0],
+                recv_sem=factor_recv.at[0],
+                device_id=(behind, c, t),
+                device_id_type=MESH,
+            )
+            for i, ref in enumerate(arrays)
+        ]
+
+    def owner_depth(side_sign, step):
+        return lax.rem(deep - side_sign * step + RING, RING)
+
+    def far_factors():
         copies = []
-        for k in range(tps):
-            span = pl.ds(k * half_rows, half_rows)
-            for i, ref in enumerate((cot_ref.at[0], qkv_ref.at[0, 1], qkv_ref.at[0, 2])):
-                copies.append(
-                    pltpu.make_async_remote_copy(
-                        src_ref=ref.at[span],
-                        dst_ref=factors.at[t, i],
-                        send_sem=factor_send,
-                        recv_sem=factor_recv,
-                        device_id=(behind, c, k),
-                        device_id_type=MESH,
+        for step in range(RING // 2, RING):
+            for half in range(2):
+                col = half * half_cols + owner_depth(sign, step) * plane_cols
+                span = pl.ds(pl.multiple_of(col, plane_cols), plane_cols)
+                for i, ref in enumerate(arrays):
+                    copies.append(
+                        pltpu.make_async_remote_copy(
+                            src_ref=ref.at[crossing, span],
+                            dst_ref=factors.at[t, i, :, span],
+                            send_sem=factor_send.at[1],
+                            recv_sem=factor_recv.at[1],
+                            device_id=(behind, c, 1 - t),
+                            device_id_type=MESH,
+                        )
                     )
-                )
         return copies
 
-    mine = filt_ref[0, pl.ds(pl.multiple_of(c * groups, groups), groups), :]
+    for load in loads[4:]:
+        load.wait()
+    mine = filt_here[...].astype(F32).reshape(groups, LANES).astype(BF16)
     lag, lane = iota((LANES, 2 * LANES), 0), iota((LANES, 2 * LANES), 1)
     taps[0] = dot(mine, (lane == LANES - lag).astype(BF16))
     taps[1] = dot(mine, (lane == lag).astype(BF16))
@@ -168,7 +219,7 @@
     lax.fori_loop(0, groups, one_band, 0)
 
     slots = ctxs * ctxs
-    dest = jnp.broadcast_to(dest_ref[pl.ds(p, 1), :], (ctxs, slots))
+    dest = jnp.broadcast_to(dest_here[pl.ds(p, 1), :], (ctxs, slots))
     entry, tile = iota((ctxs, slots), 1), iota((ctxs, slots), 0)
     slot = jnp.where(entry % ctxs == tile, dest - tile * ctxs, 0).astype(F32).astype(BF16)
     spread = (iota((slots, LANES), 0) // ctxs == iota((slots, LANES), 1) // 8).astype(BF16)
@@ -237,59 +288,130 @@
         lax.fori_loop(0, ctxs, one_tile, 0)
 
     def send_final(s):
-        half_blocks = ctxs // tps
-        for j in range(ctxs):
-            target = lax.rem(c + j, ctxs)
-            for k in range(tps):
-                pltpu.make_async_remote_copy(
-                    src_ref=outgoing.at[s, target, pl.ds(k * half_blocks, half_blocks)],
-                    dst_ref=final.at[s, t, c],
-                    send_sem=final_send.at[s],
-                    recv_sem=final_recv.at[s],
-                    device_id=(behind, target, k),
-                    device_id_type=MESH,
-                ).start()
-
+        for step in range(RING // 2):
+            for k in range(plane):
+                y = lax.rem(flat + k, plane)
+                target = lax.rem(deep + sign * step + RING, RING) * plane + y
+                piece = outgoing.at[s, target, pl.ds((1 - t) * half_blocks, half_blocks)]
+                if step == 0 and k == 0:
+                    returned[s, step * plane + flat] = outgoing[s, c, pl.ds((1 - t) * half_blocks, half_blocks)]
+                else:
+                    pltpu.make_async_remote_copy(
+                        src_ref=piece,
+                        dst_ref=returned.at[s, step * plane + flat],
+                        send_sem=return_send.at[s],
+                        recv_sem=return_recv.at[s],
+                        device_id=(p, target, t),
+                        device_id_type=MESH,
+                    ).start()
+        for step in range(RING):
+            for k in range(plane):
+                y = lax.rem(flat + k, plane)
+                target = lax.rem(deep + sign * step + RING, RING) * plane + y
+                for side in (t, 1 - t) if step >= RING // 2 else (t,):
+                    pltpu.make_async_remote_copy(
+                        src_ref=outgoing.at[s, target, pl.ds(side * half_blocks, half_blocks)],
+                        dst_ref=final.at[s, t * ctxs + c],
+                        send_sem=final_send.at[s],
+                        recv_sem=final_recv.at[s],
+                        device_id=(behind, target, side),
+                        device_id_type=MESH,
+                    ).start()
+
+    def outputs(s):
+        return ((0, 0, 0),) if s >= 2 else ((1, 2, 3), (2, 1, 2))
+
+    def ready_copies(s):
+        half = s % 2
+        copies = []
+        for step in range(RING // 2):
+            col = half * half_cols + owner_depth(sign, step) * plane_cols
+            span = pl.ds(pl.multiple_of(t * 2 * half_cols + col, plane_cols), plane_cols)
+            for out, _, _ in outputs(s):
+                copies.append(
+                    pltpu.make_async_remote_copy(
+                        src_ref=ready.at[half, step, out],
+                        dst_ref=out_ref.at[0, out, :, span],
+                        send_sem=ready_send,
+                        recv_sem=ready_recv,
+                        device_id=(behind, c, 1 - t),
+                        device_id_type=MESH,
+                    )
+                )
+        return copies
+
+    def pass_on(s):
+        half = s % 2
+        await_bytes(returned.at[s, pl.ds(0, ctxs // 2 - 1)], return_recv.at[s])
+        for step in range(RING // 2):
+
+            def one(y, carry):
+                col = half * half_cols + owner_depth(sign, step) * plane_cols + y * LANES
+                near = pl.ds(pl.multiple_of(col, LANES), LANES)
+                at = pl.ds(pl.multiple_of(y * LANES, LANES), LANES)
+                conv = returned[s, step * plane + y].astype(F32).reshape(half_rows, LANES)
+                for out, _, factor in outputs(s):
+                    value = raw[factor, crossing, near].astype(F32)
+                    ready[half, step, out, :, at] = (value * conv).astype(BF16)
+                return carry
+
+            lax.fori_loop(0, plane, one, 0)
+        for copy in ready_copies(s):
+            copy.start()
+
+    for copy in near_factors():
+        copy.start()
     for s in range(STAGES):
         await_bytes(got.at[s, pl.ds(0, ctxs - 1)], stage_recv.at[s])
         convolve(s)
         send_final(s)
         if s == 0:
-            for copy in factor_copies():
+            for copy in far_factors():
                 copy.start()
-
-    for copy in factor_copies():
-        copy.wait_send()
-    await_bytes(factors, factor_recv)
+        if s >= 1:
+            pass_on(s - 1)
+    pass_on(STAGES - 1)
+
+    await_bytes(factors.at[0], factor_recv.at[0])
+    await_bytes(factors.at[0, :, :, pl.ds(0, half_cols)], factor_recv.at[1])
 
     def finish(s):
         half = s % 2
 
-        def one(i, carry):
-            side, peer = i // ctxs, i % ctxs
-            near = pl.ds(pl.multiple_of(peer * (2 * LANES) + half * LANES, LANES), LANES)
-            far = pl.ds(
-                pl.multiple_of(side * (ctxs * 2 * LANES) + peer * (2 * LANES) + half * LANES, LANES),
-                LANES,
-            )
-            conv = final[s, side, peer].astype(F32).reshape(half_rows, LANES)
-            if s >= 2:
-                out_ref[0, 0, :, far] = (factors[side, 0, :, near].astype(F32) * conv).astype(BF16)
-            else:
-                out_ref[0, 1, :, far] = (factors[side, 2, :, near].astype(F32) * conv).astype(BF16)
-                out_ref[0, 2, :, far] = (factors[side, 1, :, near].astype(F32) * conv).astype(BF16)
+        def one(side, depth, y):
+            col = half * half_cols + depth * plane_cols + y * LANES
+            near = pl.ds(pl.multiple_of(col, LANES), LANES)
+            far = pl.ds(pl.multiple_of(side * 2 * half_cols + col, LANES), LANES)
+            conv = final[s, side * ctxs + depth * plane + y].astype(F32).reshape(half_rows, LANES)
+            for out, factor, _ in outputs(s):
+                value = factors[side, factor, :, near].astype(F32)
+                out_ref[0, out, :, far] = (value * conv).astype(BF16)
+
+        def own(i, carry):
+            one(t, i // plane, i % plane)
             return carry
 
-        lax.fori_loop(0, tps * ctxs, one, 0)
+        lax.fori_loop(0, ctxs, own, 0)
+
+        def other(i, carry):
+            one(1 - t, owner_depth(-sign, RING // 2 + i // plane), i % plane)
+            return carry
+
+        lax.fori_loop(0, ctxs // 2, other, 0)
 
     for s in range(STAGES):
-        await_bytes(final.at[s], final_recv.at[s])
+        await_bytes(final.at[s, pl.ds(0, ctxs + ctxs // 2)], final_recv.at[s])
         finish(s)
+    await_bytes(out_ref.at[0, :, :, pl.ds(0, half_cols)], ready_recv)
 
     await_bytes(marks_all.at[pl.ds(0, ctxs - 1)], mark_send)
     for s in range(STAGES):
         await_bytes(stage.at[s, pl.ds(0, ctxs - 1)], stage_send.at[s])
-        await_bytes(outgoing.at[s], final_send.at[s])
+        await_bytes(returned.at[s, pl.ds(0, ctxs // 2 - 1)], return_send.at[s])
+        await_bytes(final.at[s, pl.ds(0, ctxs + ctxs // 2)], final_send.at[s])
+    await_bytes(factors.at[0], factor_send.at[0])
+    await_bytes(factors.at[0, :, :, pl.ds(0, half_cols)], factor_send.at[1])
+    await_bytes(out_ref.at[0, :, :, pl.ds(0, half_cols)], ready_send)
 
 
 def shards(sizes, qkv_proj, cotangent, block_dest, doc_start, mr_filter):
@@ -300,13 +422,11 @@
     half_rows = rows // tps
     blocks = rows // 8
     dma = pltpu.SemaphoreType.DMA
-    anywhere = pl.BlockSpec(memory_space=pl.ANY)
-    vmem = pl.BlockSpec(memory_space=pltpu.VMEM)
     return pl.pallas_call(
         functools.partial(kernel, sizes),
         out_shape=jax.ShapeDtypeStruct((1, 3, half_rows, channels * tps), BF16),
-        in_specs=[anywhere, anywhere, vmem, vmem, vmem],
-        out_specs=vmem,
+        in_specs=[pl.BlockSpec(memory_space=pltpu.HBM)] * 5,
+        out_specs=pl.BlockSpec(memory_space=pltpu.VMEM),
         scratch_shapes=[
             pltpu.VMEM((4, rows, channels), BF16),
             pltpu.VMEM((STAGES, ctxs, blocks, 8, LANES), BF16),
@@ -321,23 +441,31 @@
             pltpu.VMEM((ctxs, LANES, LANES), BF16),
             pltpu.VMEM(((ctxs + 2) * LANES, LANES), BF16),
             pltpu.VMEM((STAGES, ctxs, blocks, 8, LANES), BF16),
-            pltpu.VMEM((STAGES, tps, ctxs, blocks // tps, 8, LANES), BF16),
+            pltpu.VMEM((STAGES, tps * ctxs, blocks // tps, 8, LANES), BF16),
+            pltpu.VMEM((STAGES, ctxs // 2, blocks // tps, 8, LANES), BF16),
+            pltpu.VMEM((2, RING // 2, 3, half_rows, ctxs // RING * LANES), BF16),
             pltpu.VMEM((tps, 3, half_rows, channels), BF16),
-            dma((4,)),
+            pltpu.VMEM(block_dest.shape, jnp.int32),
+            pltpu.VMEM((2, groups // 2, taps), BF16),
+            dma((8,)),
             dma((STAGES,)),
             dma((STAGES,)),
             dma,
             dma,
+            dma((2,)),
+            dma((2,)),
+            dma((STAGES,)),
+            dma((STAGES,)),
+            dma((STAGES,)),
+            dma((STAGES,)),
             dma,
             dma,
-            dma((STAGES,)),
-            dma((STAGES,)),
         ],
         compiler_params=pltpu.CompilerParams(
             collective_id=0, has_side_effects=True, vmem_limit_bytes=44 << 20
         ),
         name="hyena_input_grads",
-    )(qkv_proj, cotangent, block_dest, doc_start, mr_filter)
+    )(*(pltpu.with_memory_space_constraint(x, pltpu.HBM) for x in (qkv_proj, cotangent, block_dest, doc_start, mr_filter)))
 
 
 def solution(mesh):

time: 146 us -> 129 us (0.88)
  Pallas kernels: 139 us -> 127 us
  local copies, waits for them, and re-layouts: 6.97 us -> 1.67 us
    pallas_call x1, Pallas kernels: 139 us -> 127 us  [shards(): pl.pallas_call(functools.partial(kernel, sizes), out_shape=jax.ShapeDtype...]
    unnamed x11 -> x1, local copies, waits for them, and re-layouts: 6.97 us -> 1.67 us
where the time goes in v2:
time: 129 us
  Pallas kernels  127 us (98%)
  local copies, waits for them, and re-layouts  1.67 us (1%)
    pallas_call x1, Pallas kernels, shards(): pl.pallas_call(functools.partial(kernel, sizes), out_shape=jax.ShapeDtype...  127 us

profile of v2, /device:TPU:1, one launch (start us, length us, event | category | flops | bytes accessed | tf_op | source)
XLA Modules:
  0.0 129.0 jit_solution(8441268363277049260)
XLA Ops:
  0.0 127.3 %hyena_input_grads.1 = bf16[1,3,64,8192]{3,2,1,0:T(8,128)(2,1)S(1)} custom-call(bf16[1,3,128,4096]{3,2,1,0:T(8,128)(2,1)} %qkv_ref.1, bf16[1,128,4096]{2,1,0:T(8,128)(2,1)} %cot_ref.1, s32[8,256]{1,0:T(8,128)} %dest_ref.1, s32[1,128]{1,0:T(1,128)} %marks_ref.1, bf16[1,256,128]{2,1,0:T(8,128)(2,1)} %filt_ref.1), custom_call_target="tpu_custom_call" | custom-call | tf_op jit(solution)/shard_map/hyena_input_grads/pallas_call | solution.py:425
  127.3 1.7 %copy.7 = bf16[1,3,64,8192]{3,2,1,0:T(8,128)(2,1)} copy(bf16[1,3,64,8192]{3,2,1,0:T(8,128)(2,1)S(1)} %hyena_input_grads.1) | data formatting | bytes 6291456

commit v3 on v2

--- a/solution.py
+++ b/solution.py
@@ -51,6 +51,7 @@
     final,
     returned,
     ready,
+    relay,
     factors,
     dest_here,
     filt_here,
@@ -67,6 +68,9 @@
     return_recv,
     ready_send,
     ready_recv,
+    relay_send,
+    relay_recv,
+    forward_send,
 ):
     pipes, ctxs, tps = sizes
     p, c, t = lax.axis_index("pipe"), lax.axis_index("ctx"), lax.axis_index("tp")
@@ -94,6 +98,8 @@
         for k in range(tps):
             peer = (ahead, lax.rem(c + j, ctxs), k)
             pl.semaphore_signal(barrier, inc=1, device_id=peer, device_id_type=MESH)
+        peer = (behind, lax.rem(c + j, ctxs), 1 - t)
+        pl.semaphore_signal(barrier, inc=1, device_id=peer, device_id_type=MESH)
 
     loads = []
     first_group = pl.multiple_of(c * stage_groups, stage_groups)
@@ -125,26 +131,110 @@
 
         lax.fori_loop(0, ctxs, one, 0)
 
-    def stage_copy(s, j):
-        target = lax.rem(c + j, ctxs)
-        return pltpu.make_async_remote_copy(
-            src_ref=stage.at[s, target],
-            dst_ref=got.at[s, c],
-            send_sem=stage_send.at[s],
-            recv_sem=stage_recv.at[s],
-            device_id=(p, target, t),
-            device_id_type=MESH,
-        )
+    def owner_depth(side_sign, step):
+        return lax.rem(deep - side_sign * step + RING, RING)
+
+    def half_span(side):
+        return pl.ds(side * half_blocks, half_blocks)
 
     def send_stage(s):
-        for j in range(1, ctxs):
-            stage_copy(s, j).start()
+        if s < 2:
+            for step in range(RING // 2, RING):
+                span = pl.ds(owner_depth(sign, step) * plane, plane)
+                pltpu.make_async_remote_copy(
+                    src_ref=stage.at[s, span, half_span(1 - t)],
+                    dst_ref=relay.at[s, step - RING // 2],
+                    send_sem=relay_send,
+                    recv_sem=relay_recv.at[s],
+                    device_id=(behind, c, 1 - t),
+                    device_id_type=MESH,
+                ).start()
+        for step in range(RING):
+            for k in range(plane):
+                target = owner_depth(sign, step) * plane + lax.rem(flat + k, plane)
+                piece, place = stage.at[s, target], got.at[s, c]
+                if step >= RING // 2:
+                    piece, place = piece.at[half_span(t)], place.at[half_span(t)]
+                if step > 0 or k > 0:
+                    pltpu.make_async_remote_copy(
+                        src_ref=piece,
+                        dst_ref=place,
+                        send_sem=stage_send.at[s],
+                        recv_sem=stage_recv.at[s],
+                        device_id=(p, target, t),
+                        device_id_type=MESH,
+                    ).start()
         got[s, c] = stage[s, c]
 
+    def forward(s):
+        for step in range(RING // 2, RING):
+            depth = owner_depth(-sign, step)
+            if s >= 2:
+
+                def one(y, carry):
+                    near = pl.ds(
+                        pl.multiple_of(s % 2 * half_cols + depth * plane_cols + y * LANES, LANES),
+                        LANES,
+                    )
+                    key = factors[1 - t, 1, :, near].astype(F32)
+                    value = factors[1 - t, 2, :, near].astype(F32)
+                    mixed = (key * value).reshape(half_blocks, 8, LANES)
+                    relay[s, step - RING // 2, y] = mixed.astype(BF16)
+                    return carry
+
+                lax.fori_loop(0, plane, one, 0)
+            for k in range(plane):
+                y = lax.rem(flat + k, plane)
+                pltpu.make_async_remote_copy(
+                    src_ref=relay.at[s, step - RING // 2, y],
+                    dst_ref=got.at[s, c, half_span(t)],
+                    send_sem=forward_send,
+                    recv_sem=stage_recv.at[s],
+                    device_id=(ahead, depth * plane + y, 1 - t),
+                    device_id_type=MESH,
+                ).start()
+
+    arrays = (cot_ref.at[0], qkv_ref.at[0, 1], qkv_ref.at[0, 2])
+
+    def near_factors():
+        span = pl.ds(pl.multiple_of(t * half_rows, half_rows), half_rows)
+        return [
+            pltpu.make_async_remote_copy(
+                src_ref=ref.at[span],
+                dst_ref=factors.at[t, i],
+                send_sem=factor_send.at[2],
+                recv_sem=factor_recv.at[2],
+                device_id=(behind, c, t),
+                device_id_type=MESH,
+            )
+            for i, ref in enumerate(arrays)
+        ]
+
+    def far_factors(part):
+        copies = []
+        for half in range(2):
+            for step in range(RING // 2, RING):
+                col = half * half_cols + owner_depth(sign, step) * plane_cols
+                span = pl.ds(pl.multiple_of(col, plane_cols), plane_cols)
+                for i in part:
+                    copies.append(
+                        pltpu.make_async_remote_copy(
+                            src_ref=arrays[i].at[crossing, span],
+                            dst_ref=factors.at[t, i, :, span],
+                            send_sem=factor_send.at[min(i, 1)],
+                            recv_sem=factor_recv.at[min(i, 1)],
+                            device_id=(behind, c, 1 - t),
+                            device_id_type=MESH,
+                        )
+                    )
+        return copies
+
+    pl.semaphore_wait(barrier, ctxs - 1 + ctxs * tps + ctxs)
+    for copy in far_factors((1, 2)):
+        copy.start()
     loads[0].wait()
     loads[1].wait()
     products(0)
-    pl.semaphore_wait(barrier, ctxs - 1 + ctxs * tps)
     for j in range(1, ctxs):
         pltpu.make_async_remote_copy(
             src_ref=marks_ref,
@@ -163,44 +253,8 @@
     send_stage(2)
     products(3)
     send_stage(3)
-
-    arrays = (cot_ref.at[0], qkv_ref.at[0, 1], qkv_ref.at[0, 2])
-
-    def near_factors():
-        span = pl.ds(pl.multiple_of(t * half_rows, half_rows), half_rows)
-        return [
-            pltpu.make_async_remote_copy(
-                src_ref=ref.at[span],
-                dst_ref=factors.at[t, i],
-                send_sem=factor_send.at[0],
-                recv_sem=factor_recv.at[0],
-                device_id=(behind, c, t),
-                device_id_type=MESH,
-            )
-            for i, ref in enumerate(arrays)
-        ]
-
-    def owner_depth(side_sign, step):
-        return lax.rem(deep - side_sign * step + RING, RING)
-
-    def far_factors():
-        copies = []
-        for step in range(RING // 2, RING):
-            for half in range(2):
-                col = half * half_cols + owner_depth(sign, step) * plane_cols
-                span = pl.ds(pl.multiple_of(col, plane_cols), plane_cols)
-                for i, ref in enumerate(arrays):
-                    copies.append(
-                        pltpu.make_async_remote_copy(
-                            src_ref=ref.at[crossing, span],
-                            dst_ref=factors.at[t, i, :, span],
-                            send_sem=factor_send.at[1],
-                            recv_sem=factor_recv.at[1],
-                            device_id=(behind, c, 1 - t),
-                            device_id_type=MESH,
-                        )
-                    )
-        return copies
+    for copy in far_factors((0,)) + near_factors():
+        copy.start()
 
     for load in loads[4:]:
         load.wait()
@@ -217,6 +271,10 @@
         return carry
 
     lax.fori_loop(0, groups, one_band, 0)
+
+    for s in range(2):
+        await_bytes(relay.at[s], relay_recv.at[s])
+        forward(s)
 
     slots = ctxs * ctxs
     dest = jnp.broadcast_to(dest_here[pl.ds(p, 1), :], (ctxs, slots))
@@ -272,7 +330,7 @@
             source[pl.ds(at, LANES), :] = dot(to_seq[b], block).astype(BF16)
             return carry
 
-        lax.fori_loop(0, ctxs, order, 0)
+        lax.fori_loop(0, ctxs, order, 0, unroll=8)
 
         def one_tile(b, carry):
             window = source[pl.ds(pl.multiple_of((b + way) * LANES, LANES), 2 * LANES), :]
@@ -285,7 +343,7 @@
             outgoing[s, :, b] = back.reshape(ctxs, 8, LANES).astype(BF16)
             return carry
 
-        lax.fori_loop(0, ctxs, one_tile, 0)
+        lax.fori_loop(0, ctxs, one_tile, 0, unroll=4)
 
     def send_final(s):
         for step in range(RING // 2):
@@ -359,21 +417,19 @@
         for copy in ready_copies(s):
             copy.start()
 
-    for copy in near_factors():
-        copy.start()
+    await_bytes(factors.at[0, pl.ds(0, 2), :, pl.ds(0, half_cols)], factor_recv.at[1])
+    forward(2)
+    forward(3)
     for s in range(STAGES):
         await_bytes(got.at[s, pl.ds(0, ctxs - 1)], stage_recv.at[s])
         convolve(s)
         send_final(s)
-        if s == 0:
-            for copy in far_factors():
-                copy.start()
         if s >= 1:
             pass_on(s - 1)
     pass_on(STAGES - 1)
 
-    await_bytes(factors.at[0], factor_recv.at[0])
-    await_bytes(factors.at[0, :, :, pl.ds(0, half_cols)], factor_recv.at[1])
+    await_bytes(factors.at[0], factor_recv.at[2])
+    await_bytes(factors.at[0, 0, :, pl.ds(0, half_cols)], factor_recv.at[0])
 
     def finish(s):
         half = s % 2
@@ -406,11 +462,14 @@
 
     await_bytes(marks_all.at[pl.ds(0, ctxs - 1)], mark_send)
     for s in range(STAGES):
-        await_bytes(stage.at[s, pl.ds(0, ctxs - 1)], stage_send.at[s])
+        await_bytes(stage.at[s, pl.ds(0, 3 * ctxs // 4 - 1)], stage_send.at[s])
         await_bytes(returned.at[s, pl.ds(0, ctxs // 2 - 1)], return_send.at[s])
         await_bytes(final.at[s, pl.ds(0, ctxs + ctxs // 2)], final_send.at[s])
-    await_bytes(factors.at[0], factor_send.at[0])
-    await_bytes(factors.at[0, :, :, pl.ds(0, half_cols)], factor_send.at[1])
+    await_bytes(factors.at[0], factor_send.at[2])
+    await_bytes(factors.at[0, pl.ds(0, 2), :, pl.ds(0, half_cols)], factor_send.at[1])
+    await_bytes(relay.at[pl.ds(0, 2)], relay_send)
+    await_bytes(relay, forward_send)
+    await_bytes(factors.at[0, 0, :, pl.ds(0, half_cols)], factor_send.at[0])
     await_bytes(out_ref.at[0, :, :, pl.ds(0, half_cols)], ready_send)
 
 
@@ -444,6 +503,7 @@
             pltpu.VMEM((STAGES, tps * ctxs, blocks // tps, 8, LANES), BF16),
             pltpu.VMEM((STAGES, ctxs // 2, blocks // tps, 8, LANES), BF16),
             pltpu.VMEM((2, RING // 2, 3, half_rows, ctxs // RING * LANES), BF16),
+            pltpu.VMEM((STAGES, RING // 2, ctxs // RING, blocks // tps, 8, LANES), BF16),
             pltpu.VMEM((tps, 3, half_rows, channels), BF16),
             pltpu.VMEM(block_dest.shape, jnp.int32),
             pltpu.VMEM((2, groups // 2, taps), BF16),
@@ -452,13 +512,16 @@
             dma((STAGES,)),
             dma,
             dma,
-            dma((2,)),
-            dma((2,)),
+            dma((3,)),
+            dma((3,)),
             dma((STAGES,)),
             dma((STAGES,)),
             dma((STAGES,)),
             dma((STAGES,)),
             dma,
+            dma,
+            dma,
+            dma((2,)),
             dma,
         ],
         compiler_params=pltpu.CompilerParams(

time: 129 us -> 123 us (0.953)
  Pallas kernels: 127 us -> 122 us
    pallas_call x1, Pallas kernels: 127 us -> 122 us  [shards(): pl.pallas_call(functools.partial(kernel, sizes), out_shape=jax.ShapeDtype...]
where the time goes in v3:
time: 123 us
  Pallas kernels  122 us (99%)
  local copies, waits for them, and re-layouts  1.67 us (1%)
    pallas_call x1, Pallas kernels, shards(): pl.pallas_call(functools.partial(kernel, sizes), out_shape=jax.ShapeDtype...  122 us

profile of v3, /device:TPU:1, one launch (start us, length us, event | category | flops | bytes accessed | tf_op | source)
XLA Modules:
  0.0 123.4 jit_solution(18051616608051541135)
XLA Ops:
  0.0 121.7 %hyena_input_grads.1 = bf16[1,3,64,8192]{3,2,1,0:T(8,128)(2,1)S(1)} custom-call(bf16[1,3,128,4096]{3,2,1,0:T(8,128)(2,1)} %qkv_ref.1, bf16[1,128,4096]{2,1,0:T(8,128)(2,1)} %cot_ref.1, s32[8,256]{1,0:T(8,128)} %dest_ref.1, s32[1,128]{1,0:T(1,128)} %marks_ref.1, bf16[1,256,128]{2,1,0:T(8,128)(2,1)} %filt_ref.1), custom_call_target="tpu_custom_call" | custom-call | tf_op jit(solution)/shard_map/hyena_input_grads/pallas_call | solution.py:484
  121.7 1.7 %copy.7 = bf16[1,3,64,8192]{3,2,1,0:T(8,128)(2,1)} copy(bf16[1,3,64,8192]{3,2,1,0:T(8,128)(2,1)S(1)} %hyena_input_grads.1) | data formatting | bytes 6291456

commit v4 on v3

--- a/solution.py
+++ b/solution.py
@@ -91,15 +91,19 @@
     group_size = LANES // stage_groups
 
     barrier = pltpu.get_barrier_semaphore()
+    def greet(*peer):
+        pl.semaphore_signal(barrier, inc=1, device_id=peer, device_id_type=MESH)
+
     for j in range(1, ctxs):
-        peer = (p, lax.rem(c + j, ctxs), t)
-        pl.semaphore_signal(barrier, inc=1, device_id=peer, device_id_type=MESH)
+        greet(p, lax.rem(c + j, ctxs), t)
     for j in range(ctxs):
-        for k in range(tps):
-            peer = (ahead, lax.rem(c + j, ctxs), k)
-            pl.semaphore_signal(barrier, inc=1, device_id=peer, device_id_type=MESH)
-        peer = (behind, lax.rem(c + j, ctxs), 1 - t)
-        pl.semaphore_signal(barrier, inc=1, device_id=peer, device_id_type=MESH)
+        greet(ahead, lax.rem(c + j, ctxs), t)
+    greet(ahead, c, 1 - t)
+    for step in range(RING // 2, RING):
+        depth = lax.rem(deep + sign * step + RING, RING)
+        for y in range(plane):
+            greet(ahead, depth * plane + y, 1 - t)
+            greet(behind, depth * plane + y, 1 - t)
 
     loads = []
     first_group = pl.multiple_of(c * stage_groups, stage_groups)
@@ -149,7 +153,7 @@
                     device_id=(behind, c, 1 - t),
                     device_id_type=MESH,
                 ).start()
-        for step in range(RING):
+        for step in (2, 3, 1, 0):
             for k in range(plane):
                 target = owner_depth(sign, step) * plane + lax.rem(flat + k, plane)
                 piece, place = stage.at[s, target], got.at[s, c]
@@ -229,7 +233,7 @@
                     )
         return copies
 
-    pl.semaphore_wait(barrier, ctxs - 1 + ctxs * tps + ctxs)
+    pl.semaphore_wait(barrier, 3 * ctxs)
     for copy in far_factors((1, 2)):
         copy.start()
     loads[0].wait()
@@ -253,7 +257,7 @@
     send_stage(2)
     products(3)
     send_stage(3)
-    for copy in far_factors((0,)) + near_factors():
+    for copy in far_factors((0,)):
         copy.start()
 
     for load in loads[4:]:
@@ -362,7 +366,7 @@
                         device_id=(p, target, t),
                         device_id_type=MESH,
                     ).start()
-        for step in range(RING):
+        for step in (2, 3, 1, 0):
             for k in range(plane):
                 y = lax.rem(flat + k, plane)
                 target = lax.rem(deep + sign * step + RING, RING) * plane + y
@@ -413,7 +417,7 @@
                     ready[half, step, out, :, at] = (value * conv).astype(BF16)
                 return carry
 
-            lax.fori_loop(0, plane, one, 0)
+            lax.fori_loop(0, plane, one, 0, unroll=True)
         for copy in ready_copies(s):
             copy.start()
 
@@ -426,6 +430,9 @@
         send_final(s)
         if s >= 1:
             pass_on(s - 1)
+        if s == 0:
+            for copy in near_factors():
+                copy.start()
     pass_on(STAGES - 1)
 
     await_bytes(factors.at[0], factor_recv.at[2])
@@ -447,13 +454,13 @@
             one(t, i // plane, i % plane)
             return carry
 
-        lax.fori_loop(0, ctxs, own, 0)
+        lax.fori_loop(0, ctxs, own, 0, unroll=4)
 
         def other(i, carry):
             one(1 - t, owner_depth(-sign, RING // 2 + i // plane), i % plane)
             return carry
 
-        lax.fori_loop(0, ctxs // 2, other, 0)
+        lax.fori_loop(0, ctxs // 2, other, 0, unroll=4)
 
     for s in range(STAGES):
         await_bytes(final.at[s, pl.ds(0, ctxs + ctxs // 2)], final_recv.at[s])

time: 123 us -> 123 us (level)
  no operation moved by 1% of the time
where the time goes in v4:
time: 123 us
  Pallas kernels  122 us (99%)
  local copies, waits for them, and re-layouts  1.67 us (1%)
    pallas_call x1, Pallas kernels, shards(): pl.pallas_call(functools.partial(kernel, sizes), out_shape=jax.ShapeDtype...  122 us

profile of v4, /device:TPU:1, one launch (start us, length us, event | category | flops | bytes accessed | tf_op | source)
XLA Modules:
  0.0 123.4 jit_solution(9552842524241459742)
XLA Ops:
  0.0 121.7 %hyena_input_grads.1 = bf16[1,3,64,8192]{3,2,1,0:T(8,128)(2,1)S(1)} custom-call(bf16[1,3,128,4096]{3,2,1,0:T(8,128)(2,1)} %qkv_ref.1, bf16[1,128,4096]{2,1,0:T(8,128)(2,1)} %cot_ref.1, s32[8,256]{1,0:T(8,128)} %dest_ref.1, s32[1,128]{1,0:T(1,128)} %marks_ref.1, bf16[1,256,128]{2,1,0:T(8,128)(2,1)} %filt_ref.1), custom_call_target="tpu_custom_call" | custom-call | tf_op jit(solution)/shard_map/hyena_input_grads/pallas_call | solution.py:491
  121.7 1.7 %copy.7 = bf16[1,3,64,8192]{3,2,1,0:T(8,128)(2,1)} copy(bf16[1,3,64,8192]{3,2,1,0:T(8,128)(2,1)S(1)} %hyena_input_grads.1) | data formatting | bytes 6291456

commit v5 on v4

--- a/solution.py
+++ b/solution.py
@@ -233,12 +233,12 @@
                     )
         return copies
 
+    loads[0].wait()
+    loads[1].wait()
+    products(0)
     pl.semaphore_wait(barrier, 3 * ctxs)
     for copy in far_factors((1, 2)):
         copy.start()
-    loads[0].wait()
-    loads[1].wait()
-    products(0)
     for j in range(1, ctxs):
         pltpu.make_async_remote_copy(
             src_ref=marks_ref,
@@ -251,14 +251,14 @@
     send_stage(0)
     products(1)
     send_stage(1)
+    for copy in far_factors((0,)):
+        copy.start()
     loads[2].wait()
     loads[3].wait()
     products(2)
     send_stage(2)
     products(3)
     send_stage(3)
-    for copy in far_factors((0,)):
-        copy.start()
 
     for load in loads[4:]:
         load.wait()

time: 123 us -> 123 us (level)
  no operation moved by 1% of the time
where the time goes in v5:
time: 123 us
  Pallas kernels  122 us (99%)
  local copies, waits for them, and re-layouts  1.67 us (1%)
    pallas_call x1, Pallas kernels, shards(): pl.pallas_call(functools.partial(kernel, sizes), out_shape=jax.ShapeDtype...  122 us

profile of v5, /device:TPU:1, one launch (start us, length us, event | category | flops | bytes accessed | tf_op | source)
XLA Modules:
  0.0 123.4 jit_solution(7522508911867323153)
XLA Ops:
  0.0 121.7 %hyena_input_grads.1 = bf16[1,3,64,8192]{3,2,1,0:T(8,128)(2,1)S(1)} custom-call(bf16[1,3,128,4096]{3,2,1,0:T(8,128)(2,1)} %qkv_ref.1, bf16[1,128,4096]{2,1,0:T(8,128)(2,1)} %cot_ref.1, s32[8,256]{1,0:T(8,128)} %dest_ref.1, s32[1,128]{1,0:T(1,128)} %marks_ref.1, bf16[1,256,128]{2,1,0:T(8,128)(2,1)} %filt_ref.1), custom_call_target="tpu_custom_call" | custom-call | tf_op jit(solution)/shard_map/hyena_input_grads/pallas_call | solution.py:491
  121.7 1.7 %copy.7 = bf16[1,3,64,8192]{3,2,1,0:T(8,128)(2,1)} copy(bf16[1,3,64,8192]{3,2,1,0:T(8,128)(2,1)S(1)} %hyena_input_grads.1) | data formatting | bytes 6291456
